TPU v7x, 128 devices: a whole 4x4x4 slice. The times are simulated.
128 devices in a mesh: wide: 32 (over y, x, core), narrow: 4 (over z).
Axes of the slice: x: 4, y: 4, z: 4, core: 2. Of those that a mesh axis runs over, the one named last changes fastest.
Arguments:
- slab: float32 [96, 512, 8192], P('narrow', 'wide'), may hold values from -24 to 24, as said below
- start: float32 [512, 64], replicated, may hold values from -6 to 6
Outputs:
- core: float32 [96, 64, 8192], P('narrow', None, 'wide')
- factor: float32 [512, 64], replicated
Inputs may be any that keep to these rules, and one draw needn't show every extreme that they name: The slab is a planted sum of 64 separable terms plus noise.
All inputs are finite; a program needn't handle non-finite values.
Results may differ from a plain program's by a relative error of at most 0.0003.
Values sent between devices are 32-bit elements; how exact they have to be, the bound alone decides.
A program may use at most 256 MiB of HBM per device.

v0:
```python
import jax
import jax.numpy as jnp
from jax import lax
from jax.sharding import PartitionSpec as P

ITERS = 2


def orthonormal(matrix):
    product = jnp.dot(matrix.T, matrix, precision=lax.Precision.HIGHEST)
    lower = jnp.linalg.cholesky(product)
    return lax.linalg.triangular_solve(lower, matrix, left_side=False, lower=True, transpose_a=True)


def block_gram(block):
    return jnp.einsum("nix,njx->ij", block, block, precision=lax.Precision.HIGHEST)


def on_device(slab, start):
    fibres = lax.all_to_all(slab, "wide", split_axis=2, concat_axis=1, tiled=True)
    local_gram = block_gram(fibres)
    basis = orthonormal(start)
    gram = lax.psum(local_gram, ("wide", "narrow"))
    for step in range(ITERS):
        basis = orthonormal(jnp.dot(gram, basis, precision=lax.Precision.HIGHEST))
    core = jnp.einsum("ik,sif->skf", basis, fibres, precision=lax.Precision.HIGHEST)
    return (core, basis)


def solution(mesh):
    placed = (P("narrow", "wide", None), P())
    return jax.shard_map(
        on_device,
        mesh=mesh,
        in_specs=placed,
        out_specs=(P("narrow", None, "wide"), P()),
        check_vma=False,
    )
```

profile of v0, /device:TPU:1, one launch (start us, length us, event | category | flops | bytes accessed | tf_op | source)
XLA Modules:
  0.0 642.3 jit_solution(10626874872593620060)
XLA Ops:
  7.2 33.5 %copy.13 = f32[24,16,8192]{0,1,2:T(8,128)} copy(f32[24,16,8192]{2,1,0:T(8,128)} %param.5) | data formatting | bytes 25165824 | tf_op args[0]
  40.7 57.8 %reshape.27 = f32[32,1,98304]{2,1,0:T(1,128)} reshape(f32[8192,16,24]{2,1,0:T(8,128)} %bitcast.44) | data formatting | bytes 25165824
  98.5 8.6 %all-to-all-start = ((f32[32,1,98304]{2,1,0:T(1,128)}), f32[32,1,98304]{2,1,0:T(1,128)}, u32[]{:S(2)}, u32[]{:S(2)}) async-start(f32[32,1,98304]{2,1,0:T(1,128)} %reshape.27), calls=%async_computation | async-start | bytes 25165824 | tf_op jit(solution)/shard_map/all_to_all | solution.py:20
  107.2 0.3 fusion.15
  107.5 0.1 copy.15
  107.6 5.8 cholesky.59
  113.5 145.2 %all-to-all-done = f32[32,1,98304]{2,1,0:T(1,128)} async-done(((f32[32,1,98304]{2,1,0:T(1,128)}), f32[32,1,98304]{2,1,0:T(1,128)}, u32[]{:S(2)}, u32[]{:S(2)}) %all-to-all-start) | async-done | bytes 12582944 | tf_op jit(solution)/shard_map/all_to_all | solution.py:20
  258.7 0.5 broadcast.37
  259.2 36.7 %reduce.4 = f32[32,98304]{1,0:T(8,128)} reduce(f32[32,1,98304]{2,1,0:T(1,128)} %all-to-all-done, f32[]{:T(128)} %broadcast.37), dimensions={1}, to_apply=%all_to_all.13.reduce_sub_computation | reduce | bytes 25165828 | tf_op jit(solution)/shard_map/all_to_all | solution.py:20
  296.0 78.6 %reshape.28 = f32[8192,16,24]{2,1,0:T(8,128)} reshape(f32[32,98304]{1,0:T(8,128)} %reduce.4) | data formatting | bytes 25165824
  374.6 40.1 %copy.14 = f32[24,16,32,256]{3,1,2,0:T(8,128)} copy(f32[24,16,32,256]{0,1,3,2:T(8,128)} %bitcast) | data formatting | bytes 25165824 | tf_op jit(solution)/shard_map/all_to_all | solution.py:20
  414.7 24.7 %convolution_bitcast_fusion.1 = f32[512,512]{1,0:T(8,128)} fusion(f32[24,512,256]{2,1,0:T(8,128)} %bitcast.62), kind=kOutput, calls=%fused_computation.1 | convolution fusion | flops 19327352832 | bytes 13631488 | tf_op jit(solution)/shard_map/nix,njx->ij/dot_general | solution.py:16
  439.5 0.6 compare_reduce_fusion.2
  440.1 0.7 fusion.1
  440.8 4.9 custom-call.7
  445.7 0.3 convolution_bitcast_fusion.3
  446.0 147.3 %all-reduce.2.cloned.1.call-done = f32[512,512]{1,0:T(8,128)} async-done(((f32[512,512]{1,0:T(8,128)}), f32[512,512]{1,0:T(8,128)}) %all-reduce.2.cloned.1.call-update) | async-done | bytes 1048592 | tf_op jit(solution)/shard_map/psum | solution.py:23
  593.3 2.4 fusion.16
  595.7 0.3 fusion.17
  596.1 5.8 cholesky.70
  601.9 0.6 compare_reduce_fusion.1
  602.6 0.7 fusion.2
  603.3 4.9 custom-call.8
  608.1 0.3 convolution_bitcast_fusion.2
  608.5 2.4 fusion.18
  610.8 0.3 fusion.19
  611.2 5.8 cholesky.81
  617.1 0.6 compare_reduce_fusion
  617.7 0.7 fusion.3
  618.4 4.9 custom-call.9
  623.3 0.3 fusion.4
  623.6 11.8 %convolution_bitcast_fusion = f32[24,64,256]{2,1,0:T(8,128)} fusion(f32[24,512,256]{2,1,0:T(8,128)} %bitcast.63, f32[64,512]{1,0:T(8,128)S(1)} %fusion.4), kind=kOutput, calls=%fused_computation | convolution fusion | flops 2415919104 | bytes 14286848 | tf_op jit(solution)/shard_map/ik,sif->skf/dot_general | solution.py:26
  (14 shorter events, 0.3 us)
Async XLA Ops:
  7.2 100.1 %copy-start = (f32[512,64]{0,1:T(8,128)S(1)}, f32[512,64]{0,1:T(8,128)}, u32[]{:S(2)}) copy-start(f32[512,64]{0,1:T(8,128)} %param.6) | copy-start | bytes 393220
  98.5 160.2 %all-to-all-start = ((f32[32,1,98304]{2,1,0:T(1,128)}), f32[32,1,98304]{2,1,0:T(1,128)}, u32[]{:S(2)}, u32[]{:S(2)}) async-start(f32[32,1,98304]{2,1,0:T(1,128)} %reshape.27), calls=%async_computation | async-start | bytes 25165824 | tf_op jit(solution)/shard_map/all_to_all | solution.py:20
  107.2 486.2 %all-reduce.2.cloned.1.call-start = ((), (), s32[]{:S(2)}) async-start(), calls=%async_computation.1 | async-start | bytes 2097152 | tf_op jit(solution)/shard_map/psum | solution.py:23
  623.6 11.8 %copy-start.1 = (f32[64,512]{1,0:T(8,128)}, f32[64,512]{1,0:T(8,128)S(1)}, u32[]{:S(2)}) copy-start(f32[64,512]{1,0:T(8,128)S(1)} %fusion.4) | copy-start | bytes 393220
Sparse Core Ops, SparseCore 0:
  439.6 153.6 all-reduce.1
where the time goes:
time: 645 us; the launch traced here: 642 us
  waiting for transfers between devices  293 us (45%)
  local copies, waits for them, and re-layouts  211 us (33%)
  other arithmetic  73 us (11%)
  matrix products  43 us (7%)
  between operations  14.2 us (2%)
  starting transfers between devices  8.68 us (1%)
    unnamed x7, local copies, waits for them, and re-layouts  170 us
    psum x1, waiting for transfers between devices, on_device(): gram = lax.psum(local_gram, ('wide', 'narrow'))  147 us
    all_to_all x1, waiting for transfers between devices, on_device(): lax.all_to_all(slab, 'wide', split_axis=2, concat_axis=1, tiled=True)  145 us
    all_to_all x2, local copies, waits for them, and re-layouts, on_device(): lax.all_to_all(slab, 'wide', split_axis=2, concat_axis=1, tiled=True)  40.6 us
    all_to_all x1, other arithmetic, on_device(): lax.all_to_all(slab, 'wide', split_axis=2, concat_axis=1, tiled=True)  36.7 us
    dot_general x1, matrix products, block_gram(): jnp.einsum('nix,njx->ij', block, block, precision=lax.Precision.HIGHEST)  24.7 us
    another operation x9, other arithmetic, orthonormal(): lower = jnp.linalg.cholesky(product)  19.6 us
    another operation x6, other arithmetic, orthonormal(): lax.linalg.triangular_solve(lower, matrix, left_side=False, lower=True, t...  16.6 us
  transfers between devices with their start and end apart: 2, of which 2 were waited for; matrix products, arithmetic and copies ran while one was open for 2% of the time, Pallas kernels for 0%

commit v1 on v0

v1 whole, which is shorter than its diff:
```python
import jax
import jax.numpy as jnp
from jax import lax
from jax.experimental import pallas as pl
from jax.experimental.pallas import tpu as pltpu
from jax.sharding import PartitionSpec as P

MESH = pl.DeviceIdType.MESH
F32, BF16 = jnp.float32, jnp.bfloat16
ITERS = 2
NX, NY, CORES, NZ = 4, 4, 2, 4
WIDE = NX * NY * CORES
PEERS = [(y, x, c) for y in range(NY) for x in range(NX) for c in range(CORES) if (y, x, c) != (0, 0, 0)]


def dot(a, b, dims=((1,), (0,)), exact=True):
    precision = lax.Precision.HIGHEST if exact else None
    return lax.dot_general(a, b, (dims, ((), ())), precision=precision, preferred_element_type=F32)


def split(x):
    high = x.astype(BF16)
    return high, (x - high.astype(F32)).astype(BF16)


def inverse_factor(gram2):
    n = gram2.shape[0]
    row = lax.broadcasted_iota(jnp.int32, (n, 2 * n), 0)
    lane = lax.broadcasted_iota(jnp.int32, (n, 2 * n), 1)
    work = jnp.where(lane < n, jnp.concatenate([gram2, gram2], axis=1), (lane - n == row).astype(F32))

    def step(k, work):
        pivot_row = jnp.sum(jnp.where(row == k, work, 0.0), axis=0, keepdims=True)
        column = jnp.sum(jnp.where(lane == k, work, 0.0), axis=1, keepdims=True)
        pivot = jnp.sum(jnp.where(lane[:1] == k, pivot_row, 0.0), axis=1, keepdims=True)
        scale = 1.0 / jnp.sqrt(pivot)
        scaled = pivot_row * scale
        return jnp.where(row == k, scaled, jnp.where(row > k, work - (column * scale) * scaled, work))

    work = lax.fori_loop(0, n, step, work)
    return work[:, n:]


def orthonormal(zp):
    both = dot(zp, zp, ((0,), (0,)))
    inv_t = inverse_factor(both[:64, :64] + both[64:, 64:]).T
    zero = jnp.zeros_like(inv_t)
    blocks = jnp.concatenate(
        [jnp.concatenate([inv_t, zero], axis=1), jnp.concatenate([zero, inv_t], axis=1)], axis=0)
    return dot(zp, blocks)


def kernel(x_ref, start_ref, core_ref, factor_ref, buf, high, low, gram, out_buf, zsend, zslots, zz, zall,
           own_sem, send_sem, recv_sem, out_sem, zsend_sem, rs_sem, zz_send_sem, zz_sem, ag_send_sem, ag_sem):
    w = lax.axis_index("wide")
    z = lax.axis_index("narrow")
    cc, xx, yy = lax.rem(w, CORES), lax.rem(w // CORES, NX), w // (CORES * NX)
    spectra, rows, cols = buf.shape[0], x_ref.shape[1], buf.shape[2]

    def peer(offset):
        y, x, c = offset
        return (lax.rem(yy + y, NY) * NX + lax.rem(xx + x, NX)) * CORES + lax.rem(cc + c, CORES)

    peers = [peer(offset) for offset in PEERS]
    depths = [lax.rem(z + d, NZ) for d in range(1, NZ)]

    barrier = pltpu.get_barrier_semaphore()
    for t in peers:
        pl.semaphore_signal(barrier, inc=1, device_id=(t, z), device_id_type=MESH)
    for d in depths:
        pl.semaphore_signal(barrier, inc=1, device_id=(w, d), device_id_type=MESH)
    pl.semaphore_wait(barrier, len(peers) + len(depths))

    def block(ref, t):
        return ref.at[:, pl.ds(pl.multiple_of(t * cols, cols), cols)]

    my_rows = pl.ds(pl.multiple_of(w * rows, rows), rows)

    @pl.loop(0, spectra)
    def _(s):
        for t in peers:
            pltpu.make_async_remote_copy(
                src_ref=block(x_ref.at[s], t), dst_ref=buf.at[s, my_rows, :],
                send_sem=send_sem, recv_sem=recv_sem.at[s], device_id=(t, z), device_id_type=MESH).start()

    own = pltpu.make_async_copy(
        x_ref.at[:, :, pl.ds(pl.multiple_of(w * cols, cols), cols)], buf.at[:, my_rows, :], own_sem)
    own.start()

    start = start_ref[...]
    basis = orthonormal(jnp.concatenate([start[:256], start[256:]], axis=1))
    gram[...] = jnp.zeros_like(gram)
    own.wait()

    def arrived(ref, sem):
        pltpu.make_async_copy(ref, ref, sem).wait()

    @pl.loop(0, spectra)
    def _(s):
        arrived(buf.at[s, pl.ds(0, len(PEERS) * rows), :], recv_sem.at[s])
        h, l = split(buf[s])
        high[s] = h
        low[s] = l
        nt = ((1,), (1,))
        gram[...] += (dot(h, h, nt, False) + dot(h, l, nt, False)) + (dot(l, h, nt, False) + dot(l, l, nt, False))

    for it in range(ITERS):
        top, bottom = basis[:, :64], basis[:, 64:]
        parts = [dot(gram[pl.ds(r, 256), pl.ds(0, 256)], top) + dot(gram[pl.ds(r, 256), pl.ds(256, 256)], bottom)
                 for r in (0, 256)]
        zsend[it] = jnp.concatenate(parts, axis=1)
        for t in peers:
            pltpu.make_async_remote_copy(
                src_ref=zsend.at[it, pl.ds(pl.multiple_of(t * 8, 8), 8), :], dst_ref=zslots.at[it, w],
                send_sem=zsend_sem.at[it], recv_sem=rs_sem.at[it], device_id=(t, z), device_id_type=MESH).start()
        zslots[it, w] = zsend[it, pl.ds(pl.multiple_of(w * 8, 8), 8), :]
        arrived(zslots.at[it, pl.ds(0, len(PEERS))], rs_sem.at[it])
        zz[it, z] = jnp.sum(zslots[it], axis=0)
        for d in depths:
            pltpu.make_async_remote_copy(
                src_ref=zz.at[it, z], dst_ref=zz.at[it, z],
                send_sem=zz_send_sem.at[it], recv_sem=zz_sem.at[it], device_id=(w, d), device_id_type=MESH).start()
        arrived(zz.at[it, pl.ds(0, len(depths))], zz_sem.at[it])
        mine = pl.ds(pl.multiple_of(w * 8, 8), 8)
        zall[it, mine, :] = (zz[it, 0] + zz[it, 1]) + (zz[it, 2] + zz[it, 3])
        for t in peers:
            pltpu.make_async_remote_copy(
                src_ref=zall.at[it, mine, :], dst_ref=zall.at[it, mine, :],
                send_sem=ag_send_sem.at[it], recv_sem=ag_sem.at[it], device_id=(t, z), device_id_type=MESH).start()
        arrived(zall.at[it, pl.ds(0, len(PEERS) * 8), :], ag_sem.at[it])
        basis = orthonormal(zall[it])

    factor_ref[0:256, :] = basis[:, :64]
    factor_ref[256:512, :] = basis[:, 64:]
    basis_t = basis.T
    bh, bl = split(jnp.concatenate([basis_t[:64], basis_t[64:]], axis=1))
    both = jnp.concatenate([bh, bl], axis=0)

    @pl.loop(0, spectra)
    def _(s):
        wide = dot(both, high[s], exact=False)
        out_buf[s] = (wide[:64] + wide[64:]) + dot(bh, low[s], exact=False)
        pltpu.make_async_copy(out_buf.at[s], core_ref.at[s], out_sem).start()

    arrived(buf.at[:, pl.ds(0, len(PEERS) * rows), :], send_sem)
    for it in range(ITERS):
        arrived(zslots.at[it, pl.ds(0, len(PEERS))], zsend_sem.at[it])
        arrived(zz.at[it, pl.ds(0, len(depths))], zz_send_sem.at[it])
        arrived(zall.at[it, pl.ds(0, len(PEERS) * 8), :], ag_send_sem.at[it])
    arrived(out_buf, out_sem)


def on_device(slab, start):
    spectra, rows, columns = slab.shape
    cols = columns // WIDE
    dma = pltpu.SemaphoreType.DMA
    return pl.pallas_call(
        kernel,
        out_shape=(jax.ShapeDtypeStruct((spectra, 64, cols), F32), jax.ShapeDtypeStruct((512, 64), F32)),
        in_specs=[pl.BlockSpec(memory_space=pltpu.HBM), pl.BlockSpec(memory_space=pltpu.VMEM)],
        out_specs=(pl.BlockSpec(memory_space=pltpu.HBM), pl.BlockSpec(memory_space=pltpu.VMEM)),
        scratch_shapes=[
            pltpu.VMEM((spectra, 512, cols), F32),
            pltpu.VMEM((spectra, 512, cols), BF16),
            pltpu.VMEM((spectra, 512, cols), BF16),
            pltpu.VMEM((512, 512), F32),
            pltpu.VMEM((spectra, 64, cols), F32),
            pltpu.VMEM((ITERS, 256, 128), F32),
            pltpu.VMEM((ITERS, WIDE, 8, 128), F32),
            pltpu.VMEM((ITERS, NZ, 8, 128), F32),
            pltpu.VMEM((ITERS, 256, 128), F32),
            dma(()), dma(()), dma((spectra,)), dma(()),
            dma((ITERS,)), dma((ITERS,)), dma((ITERS,)), dma((ITERS,)), dma((ITERS,)), dma((ITERS,)),
        ],
        compiler_params=pltpu.CompilerParams(
            collective_id=0, has_side_effects=True, vmem_limit_bytes=56 * 2**20),
    )(slab, start)


def solution(mesh):
    return jax.shard_map(
        on_device,
        mesh=mesh,
        in_specs=(P("narrow", "wide", None), P()),
        out_specs=(P("narrow", None, "wide"), P()),
        check_vma=False,
    )
```

time: 645 us -> 209 us (0.32)
  waiting for transfers between devices: 293 us -> 0 us
  local copies, waits for them, and re-layouts: 211 us -> 6.16 us
  Pallas kernels: 0 us -> 202 us
  other arithmetic: 73 us -> 0 us
  matrix products: 43 us -> 0 us
  between operations: 14.2 us -> 0.64 us
  starting transfers between devices: 8.68 us -> 0 us
    pallas_call x0 -> x1, Pallas kernels: none -> 202 us  [on_device(): pl.pallas_call(kernel, out_shape=(jax.ShapeDtypeStruct((spectra, 64, cols...]
    unnamed x7 -> x2, local copies, waits for them, and re-layouts: 170 us -> 4.44 us
    psum x1 -> x0, waiting for transfers between devices: 147 us -> none  [on_device(): gram = lax.psum(local_gram, ('wide', 'narrow'))]
    all_to_all x1 -> x0, waiting for transfers between devices: 145 us -> none  [on_device(): lax.all_to_all(slab, 'wide', split_axis=2, concat_axis=1, tiled=True)]
    dot_general x7 -> x0, matrix products: 42 us -> none  [the longest x1 24.7 us: block_gram(): jnp.einsum('nix,njx->ij', block, block, precision=lax.Precision.HIGHEST)]
    all_to_all x2 -> x0, local copies, waits for them, and re-layouts: 40.6 us -> none  [on_device(): lax.all_to_all(slab, 'wide', split_axis=2, concat_axis=1, tiled=True)]
    all_to_all x1 -> x0, other arithmetic: 36.7 us -> none  [on_device(): lax.all_to_all(slab, 'wide', split_axis=2, concat_axis=1, tiled=True)]
    another operation x15 -> x0, other arithmetic: 36.2 us -> none  [the longest x9 19.6 us: orthonormal(): lower = jnp.linalg.cholesky(product)]
  transfers between devices with their start and end apart: 2 -> 0, of which waited for: 2 -> 0; matrix products, arithmetic and copies ran while one was open for 2% -> 0% of each run, Pallas kernels for 0% -> 0%
where the time goes in v1:
time: 209 us
  Pallas kernels  202 us (97%)
  local copies, waits for them, and re-layouts  6.16 us (3%)
    pallas_call x1, Pallas kernels, on_device(): pl.pallas_call(kernel, out_shape=(jax.ShapeDtypeStruct((spectra, 64, cols...  202 us
    unnamed x2, local copies, waits for them, and re-layouts  4.44 us

profile of v1, /device:TPU:1, one launch (start us, length us, event | category | flops | bytes accessed | tf_op | source)
XLA Modules:
  0.0 208.9 jit_solution(13029477244315643877)
XLA Ops:
  0.6 1.7 copy.4.start_ref
  2.4 202.1 %shard_map.41 = (f32[24,64,256]{2,1,0:T(8,128)}, f32[512,64]{1,0:T(8,128)}) custom-call(f32[24,16,8192]{2,1,0:T(8,128)} %x_ref.1, f32[512,64]{1,0:T(8,128)} %copy.4.start_ref), custom_call_target="tpu_custom_call" | custom-call | tf_op jit(solution)/shard_map/pallas_call | solution.py:157
  204.5 1.7 copy.5
  206.2 2.7 %copy.7 = f32[24,64,256]{2,1,0:T(8,128)} copy(f32[24,64,256]{2,1,0:T(8,128)} %get-tuple-element.6) | data formatting | bytes 3145728

commit v2 on v1

v2 whole, which is shorter than its diff:
```python
import jax
import jax.numpy as jnp
from jax import lax
from jax.experimental import pallas as pl
from jax.experimental.pallas import tpu as pltpu
from jax.sharding import PartitionSpec as P

MESH = pl.DeviceIdType.MESH
F32, BF16 = jnp.float32, jnp.bfloat16
ITERS = 2
AHEAD = 8
PARTS = 2
GROUP = 8
KERNEL_VMEM = 40 * 2**20
PROJECT_VMEM = 8 * 2**20
NX, NY, CORES, NZ = 4, 4, 2, 4
WIDE = NX * NY * CORES
PEERS = [(y, x, c) for y in range(NY) for x in range(NX) for c in range(CORES) if (y, x, c) != (0, 0, 0)]


def dot(a, b, dims=((1,), (0,)), exact=True):
    precision = lax.Precision.HIGHEST if exact else None
    return lax.dot_general(a, b, (dims, ((), ())), precision=precision, preferred_element_type=F32)


def split(x):
    high = x.astype(BF16)
    return high, (x - high.astype(F32)).astype(BF16)


def inverse_factor(gram2):
    n = gram2.shape[0]
    sub = lax.broadcasted_iota(jnp.int32, (8, 2 * n), 0)
    lane = lax.broadcasted_iota(jnp.int32, (8, 2 * n), 1)
    doubled = jnp.concatenate([gram2, gram2], axis=1)
    work = [jnp.where(lane < n, doubled[8 * i:8 * i + 8], (lane - n == sub + 8 * i).astype(F32)) for i in range(n // 8)]

    def spread(x):
        return jnp.broadcast_to(x, (8, 2 * n))

    for k in range(0, n, 4):
        b, j = divmod(k, 8)
        pivot = work[b]
        r = [spread(pivot[j + t:j + t + 1]) for t in range(4)]
        e = [[spread(pivot[j + t:j + t + 1, k + u:k + u + 1]) for u in range(t + 1)] for t in range(4)]
        inv0 = 1.0 / (e[0][0] * e[1][1] - e[1][0] * e[1][0])
        y0 = (e[1][1] * r[0] - e[1][0] * r[1]) * inv0
        y1 = (e[0][0] * r[1] - e[1][0] * r[0]) * inv0
        r2 = r[2] - (e[2][0] * y0 + e[2][1] * y1)
        r3 = r[3] - (e[3][0] * y0 + e[3][1] * y1)

        def reduced(t, u):
            return e[t][u] - (e[1][1] * e[u][0] * e[t][0] - e[1][0] * (e[u][1] * e[t][0] + e[u][0] * e[t][1])
                              + e[0][0] * e[u][1] * e[t][1]) * inv0

        p, q, v = reduced(2, 2), reduced(3, 2), reduced(3, 3)
        inv1 = 1.0 / (p * v - q * q)
        y2 = (v * r2 - q * r3) * inv1
        y3 = (p * r3 - q * r2) * inv1
        f = [[spread(y[:1, k + t:k + t + 1]) for y in (y0, y1)] for t in (2, 3)]
        work[b] = jnp.where(sub == j + 2, r2, jnp.where(sub == j + 3, r3, pivot))
        for i in range(b, n // 8):
            if i == b and j == 4:
                continue
            source = pivot if i == b else work[i]
            c = [spread(source[:, k + t:k + t + 1]) for t in range(4)]
            c2 = c[2] - (c[0] * f[0][0] + c[1] * f[0][1])
            c3 = c[3] - (c[0] * f[1][0] + c[1] * f[1][1])
            update = (c[0] * y0 + c[1] * y1) + (c2 * y2 + c3 * y3)
            work[i] = work[i] - (jnp.where(sub > j + 3, update, 0.0) if i == b else update)

    odd = sub % 2 == 1
    rows = []
    for i in range(n // 8):
        first = sub - sub % 2 + 8 * i
        before = jnp.concatenate([work[i][7:8], work[i][:7]], axis=0)
        here = jnp.where(lane == first, work[i], 0.0)
        q = jnp.sum(jnp.where(odd, here, 0.0), axis=1, keepdims=True)
        p = jnp.sum(jnp.where(odd, jnp.where(lane == first, before, 0.0), here), axis=1, keepdims=True)
        v = jnp.sum(jnp.where(jnp.logical_and(odd, lane == first + 1), work[i], 0.0), axis=1, keepdims=True)
        m = q / p
        rows.append((work[i] - m * before) / jnp.sqrt(jnp.where(odd[:, :1], v - q * m, p)))
    return jnp.concatenate(rows, axis=0)[:, n:]


def inverse_of(zt):
    c = dot(zt, zt, ((1,), (1,)))
    n = c.shape[0]
    on = lax.broadcasted_iota(jnp.int32, (n, n), 0) == lax.broadcasted_iota(jnp.int32, (n, n), 1)
    diagonal = jnp.where(on, c, 0.0)
    down = 1.0 / jnp.sqrt(jnp.sum(diagonal, axis=1, keepdims=True))
    across = 1.0 / jnp.sqrt(jnp.sum(diagonal, axis=0, keepdims=True))
    return inverse_factor((c * down) * across) * across


def fold(stacked):
    return stacked[:64] + stacked[64:]


def split3(x):
    high = x.astype(BF16)
    rest = x - high.astype(F32)
    middle = rest.astype(BF16)
    return high, middle, (rest - middle.astype(F32)).astype(BF16)


def kernel(x_ref, start_ref, high, low, basis_ref, start_buf, buf, gram, pair, zacc, g3, zsend, zslots, zz, zall,
           start_sem, own_sem, send_sem, recv_sem, zsend_sem, rs_sem, zz_send_sem, zz_sem, ag_send_sem, ag_sem):
    w = lax.axis_index("wide")
    z = lax.axis_index("narrow")
    cc, xx, yy = lax.rem(w, CORES), lax.rem(w // CORES, NX), w // (CORES * NX)
    spectra, rows, cols = buf.shape[0], x_ref.shape[1], buf.shape[2]

    def peer(offset):
        y, x, c = offset
        return (lax.rem(yy + y, NY) * NX + lax.rem(xx + x, NX)) * CORES + lax.rem(cc + c, CORES)

    peers = [peer(offset) for offset in PEERS]
    far_first = [peer(offset) for offset in sorted(PEERS, key=lambda o: -min(o[0], NY - o[0]) - min(o[1], NX - o[1]))]
    depths = [lax.rem(z + d, NZ) for d in (2, 1, 3)]

    barrier = pltpu.get_barrier_semaphore()
    for t in far_first:
        pl.semaphore_signal(barrier, inc=1, device_id=(t, z), device_id_type=MESH)
    for d in depths:
        pl.semaphore_signal(barrier, inc=1, device_id=(w, d), device_id_type=MESH)
    my_rows = pl.ds(pl.multiple_of(w * rows, rows), rows)
    own = pltpu.make_async_copy(
        x_ref.at[:, :, pl.ds(pl.multiple_of(w * cols, cols), cols)], buf.at[:, my_rows, :], own_sem)
    own.start()
    begun = pltpu.make_async_copy(start_ref, start_buf, start_sem)
    begun.start()
    pl.semaphore_wait(barrier, len(peers) + len(depths))

    part = rows // PARTS

    def send(s):
        for r in range(PARTS):
            here = pl.ds(pl.multiple_of(w * rows + r * part, part), part)
            for t in peers:
                pltpu.make_async_remote_copy(
                    src_ref=x_ref.at[s, pl.ds(r * part, part), pl.ds(pl.multiple_of(t * cols, cols), cols)],
                    dst_ref=buf.at[s, here, :],
                    send_sem=send_sem, recv_sem=recv_sem.at[s], device_id=(t, z), device_id_type=MESH).start()

    def arrived(ref, sem):
        pltpu.make_async_copy(ref, ref, sem).wait()

    nt = ((1,), (1,))

    def multiply(s):
        arrived(buf.at[s, pl.ds(0, len(PEERS) * rows), :], recv_sem.at[s])
        h, l = split(buf[s])
        high[s] = h
        low[s] = l
        inner = jnp.concatenate(split(fold(dot(pair[...], h, exact=False) + dot(pair[...], l, exact=False))), axis=0)
        zacc[...] += fold(dot(inner, h, nt, False) + dot(inner, l, nt, False))

    def accumulate(s):
        h, l = high[s], low[s]
        gram[...] += (dot(h, h, nt, False) + dot(h, l, nt, False)) + (dot(l, h, nt, False) + dot(l, l, nt, False))

    @pl.loop(0, AHEAD)
    def _(s):
        send(s)

    gram[...] = jnp.zeros_like(gram)
    zacc[...] = jnp.zeros_like(zacc)
    begun.wait()
    start = start_buf[...]
    pair[...] = jnp.concatenate(split(dot(inverse_of(start), start)), axis=0)
    own.wait()

    @pl.loop(0, spectra - AHEAD)
    def _(s):
        send(s + AHEAD)
        multiply(s)
        accumulate(s)

    @pl.loop(spectra - AHEAD, spectra - 1)
    def _(s):
        multiply(s)
        accumulate(s)

    multiply(spectra - 1)

    def tile(ref, t):
        return ref.at[pl.ds(pl.multiple_of(t // 4 * 8, 8), 8), pl.ds(pl.multiple_of(lax.rem(t, 4) * 128, 128), 128)]

    def reduce(it, value):
        zsend[it] = value
        for t in far_first:
            pltpu.make_async_remote_copy(
                src_ref=tile(zsend.at[it], t), dst_ref=zslots.at[it, w],
                send_sem=zsend_sem.at[it], recv_sem=rs_sem.at[it], device_id=(t, z), device_id_type=MESH).start()
        zslots[it, w] = tile(zsend.at[it], w)[...]

    def spread(it):
        arrived(zslots.at[it, pl.ds(0, len(PEERS))], rs_sem.at[it])
        zz[it, z] = jnp.sum(zslots[it], axis=0)
        for d in depths:
            pltpu.make_async_remote_copy(
                src_ref=zz.at[it, z], dst_ref=zz.at[it, z],
                send_sem=zz_send_sem.at[it], recv_sem=zz_sem.at[it], device_id=(w, d), device_id_type=MESH).start()
        arrived(zz.at[it, pl.ds(0, len(depths))], zz_sem.at[it])
        tile(zall.at[it], w)[...] = (zz[it, 0] + zz[it, 1]) + (zz[it, 2] + zz[it, 3])
        for t in far_first:
            pltpu.make_async_remote_copy(
                src_ref=tile(zall.at[it], w), dst_ref=tile(zall.at[it], w),
                send_sem=ag_send_sem.at[it], recv_sem=ag_sem.at[it], device_id=(t, z), device_id_type=MESH).start()

    def gathered(it):
        arrived(zslots.at[it, pl.ds(0, len(PEERS))], ag_sem.at[it])
        return zall[it]

    reduce(0, zacc[...])
    accumulate(spectra - 1)
    for i, g in enumerate(split3(gram[...])):
        g3[i] = g
    spread(0)
    z1 = gathered(0)
    zh, zm, zl = split3(z1)
    by_high = dot(jnp.concatenate([zh, zm, zl], axis=0), g3[0], exact=False)
    by_middle = dot(jnp.concatenate([zh, zm], axis=0), g3[1], exact=False)
    by_low = dot(zh, g3[2], exact=False)
    reduce(1, by_high[:64] + ((by_high[64:128] + by_middle[:64]) + ((by_high[128:] + by_middle[64:]) + by_low)))
    inv1 = inverse_of(z1)
    spread(1)
    z2 = dot(inv1, gathered(1))
    basis_ref[...] = dot(inverse_of(z2), z2)

    arrived(buf.at[:, pl.ds(0, len(PEERS) * rows), :], send_sem)
    for it in range(ITERS):
        arrived(zslots.at[it, pl.ds(0, len(PEERS))], zsend_sem.at[it])
        arrived(zz.at[it, pl.ds(0, len(depths))], zz_send_sem.at[it])
        arrived(zslots.at[it, pl.ds(0, len(PEERS))], ag_send_sem.at[it])


def project(high, low, basis_ref, core_ref, factor_ref):
    basis = basis_ref[...]
    bh, bl = split(basis)
    both = jnp.concatenate([bh, bl], axis=0)
    step = pl.program_id(0)

    @pl.when(step == 0)
    def _():
        factor_ref[...] = basis

    for i in range(core_ref.shape[0]):
        s = step * core_ref.shape[0] + i
        core_ref[i] = fold(dot(both, high[s], exact=False)) + dot(bh, low[s], exact=False)


def on_device(slab, start):
    spectra, rows, columns = slab.shape
    cols = columns // WIDE
    dma = pltpu.SemaphoreType.DMA
    vmem = pl.BlockSpec(memory_space=pltpu.VMEM)
    hbm = pl.BlockSpec(memory_space=pltpu.HBM)
    high, low, basis = pl.pallas_call(
        kernel,
        out_shape=(pltpu.VMEM((spectra, 512, cols), BF16), pltpu.VMEM((spectra, 512, cols), BF16),
                   pltpu.VMEM((64, 512), F32)),
        in_specs=[hbm, hbm],
        out_specs=(vmem, vmem, vmem),
        scratch_shapes=[
            pltpu.VMEM((64, 512), F32),
            pltpu.VMEM((spectra, 512, cols), F32),
            pltpu.VMEM((512, 512), F32),
            pltpu.VMEM((128, 512), BF16),
            pltpu.VMEM((64, 512), F32),
            pltpu.VMEM((3, 512, 512), BF16),
            pltpu.VMEM((ITERS, 64, 512), F32),
            pltpu.VMEM((ITERS, WIDE, 8, 128), F32),
            pltpu.VMEM((ITERS, NZ, 8, 128), F32),
            pltpu.VMEM((ITERS, 64, 512), F32),
            dma(()), dma(()), dma(()), dma((spectra,)),
            dma((ITERS,)), dma((ITERS,)), dma((ITERS,)), dma((ITERS,)), dma((ITERS,)), dma((ITERS,)),
        ],
        compiler_params=pltpu.CompilerParams(
            collective_id=0, has_side_effects=True, vmem_limit_bytes=KERNEL_VMEM),
    )(slab, start.T)
    core, factor_t = pl.pallas_call(
        project,
        grid=(spectra // GROUP,),
        out_shape=(jax.ShapeDtypeStruct((spectra, 64, cols), F32), jax.ShapeDtypeStruct((64, 512), F32)),
        in_specs=[vmem, vmem, vmem],
        out_specs=(pl.BlockSpec((GROUP, 64, cols), lambda g: (g, 0, 0)), pl.BlockSpec((64, 512), lambda g: (0, 0))),
        compiler_params=pltpu.CompilerParams(vmem_limit_bytes=PROJECT_VMEM),
    )(high, low, basis)
    return core, factor_t.T


def solution(mesh):
    return jax.shard_map(
        on_device,
        mesh=mesh,
        in_specs=(P("narrow", "wide", None), P()),
        out_specs=(P("narrow", None, "wide"), P()),
        check_vma=False,
    )
```

time: 209 us -> 187 us (0.89)
  Pallas kernels: 202 us -> 185 us
  local copies, waits for them, and re-layouts: 6.16 us -> 0.9 us
    pallas_call x1 -> x2, Pallas kernels: 202 us -> 185 us  [the longest x1 182 us: on_device(): pl.pallas_call(kernel, out_shape=(pltpu.VMEM((spectra, 512, cols), BF16),...]
    unnamed x2, local copies, waits for them, and re-layouts: 4.44 us -> 0.9 us
where the time goes in v2:
time: 187 us
  Pallas kernels  185 us (99%)
    pallas_call x1, Pallas kernels, on_device(): pl.pallas_call(kernel, out_shape=(pltpu.VMEM((spectra, 512, cols), BF16),...  182 us

profile of v2, /device:TPU:1, one launch (start us, length us, event | category | flops | bytes accessed | tf_op | source)
XLA Modules:
  0.0 187.0 jit_solution(1477037187767648702)
XLA Ops:
  0.6 0.0 copy-start
  0.6 0.9 copy-done
  1.5 182.1 %shard_map.41 = (bf16[24,512,256]{2,1,0:T(8,128)(2,1)S(1)}, bf16[24,512,256]{2,1,0:T(8,128)(2,1)S(1)}, f32[64,512]{1,0:T(8,128)S(1)}) custom-call(f32[24,16,8192]{2,1,0:T(8,128)} %x_ref.1, f32[64,512]{1,0:T(8,128)S(1)} %bitcast.2), custom_call_target="tpu_custom_call" | custom-call | tf_op jit(solution)/shard_map/pallas_call | solution.py:260
  183.6 3.4 %shard_map.42 = (f32[24,64,256]{2,1,0:T(8,128)}, f32[64,512]{1,0:T(8,128)}) custom-call(bf16[24,512,256]{2,1,0:T(8,128)(2,1)S(1)} %get-tuple-element.7.high, bf16[24,512,256]{2,1,0:T(8,128)(2,1)S(1)} %get-tuple-element.8.low, f32[64,512]{1,0:T(8,128)S(1)} %get-tuple-element.9.basis_ref), custom_call_target="tpu_custom_call" | custom-call | tf_op jit(solution)/shard_map/pallas_call | solution.py:283
Async XLA Ops:
  0.6 0.9 copy-start

commit v3 on v2

--- a/solution.py
+++ b/solution.py
@@ -11,7 +11,7 @@
 AHEAD = 8
 PARTS = 2
 GROUP = 8
-KERNEL_VMEM = 40 * 2**20
+KERNEL_VMEM = 52953088
 PROJECT_VMEM = 8 * 2**20
 NX, NY, CORES, NZ = 4, 4, 2, 4
 WIDE = NX * NY * CORES
@@ -38,36 +38,32 @@
     def spread(x):
         return jnp.broadcast_to(x, (8, 2 * n))
 
-    for k in range(0, n, 4):
-        b, j = divmod(k, 8)
-        pivot = work[b]
-        r = [spread(pivot[j + t:j + t + 1]) for t in range(4)]
-        e = [[spread(pivot[j + t:j + t + 1, k + u:k + u + 1]) for u in range(t + 1)] for t in range(4)]
-        inv0 = 1.0 / (e[0][0] * e[1][1] - e[1][0] * e[1][0])
-        y0 = (e[1][1] * r[0] - e[1][0] * r[1]) * inv0
-        y1 = (e[0][0] * r[1] - e[1][0] * r[0]) * inv0
-        r2 = r[2] - (e[2][0] * y0 + e[2][1] * y1)
-        r3 = r[3] - (e[3][0] * y0 + e[3][1] * y1)
-
-        def reduced(t, u):
-            return e[t][u] - (e[1][1] * e[u][0] * e[t][0] - e[1][0] * (e[u][1] * e[t][0] + e[u][0] * e[t][1])
-                              + e[0][0] * e[u][1] * e[t][1]) * inv0
-
-        p, q, v = reduced(2, 2), reduced(3, 2), reduced(3, 3)
-        inv1 = 1.0 / (p * v - q * q)
-        y2 = (v * r2 - q * r3) * inv1
-        y3 = (p * r3 - q * r2) * inv1
-        f = [[spread(y[:1, k + t:k + t + 1]) for y in (y0, y1)] for t in (2, 3)]
-        work[b] = jnp.where(sub == j + 2, r2, jnp.where(sub == j + 3, r3, pivot))
-        for i in range(b, n // 8):
-            if i == b and j == 4:
-                continue
-            source = pivot if i == b else work[i]
-            c = [spread(source[:, k + t:k + t + 1]) for t in range(4)]
-            c2 = c[2] - (c[0] * f[0][0] + c[1] * f[0][1])
-            c3 = c[3] - (c[0] * f[1][0] + c[1] * f[1][1])
-            update = (c[0] * y0 + c[1] * y1) + (c2 * y2 + c3 * y3)
-            work[i] = work[i] - (jnp.where(sub > j + 3, update, 0.0) if i == b else update)
+    for b in range(n // 8):
+        k = 8 * b
+        later = range(b + 1, n // 8)
+        row = [spread(work[b][t:t + 1]) for t in range(8)]
+        e = [[spread(work[b][t:t + 1, k + u:k + u + 1]) for u in range(t + 1)] for t in range(8)]
+        column = {i: [spread(work[i][:, k + u:k + u + 1]) for u in range(8)] for i in later}
+        update = {i: 0.0 for i in later}
+        for p in range(0, 8, 2):
+            aa, ab, bb = e[p][p], e[p + 1][p], e[p + 1][p + 1]
+            inv = 1.0 / (aa * bb - ab * ab)
+            y0 = (bb * row[p] - ab * row[p + 1]) * inv
+            y1 = (aa * row[p + 1] - ab * row[p]) * inv
+            f = {t: ((bb * e[t][p] - ab * e[t][p + 1]) * inv, (aa * e[t][p + 1] - ab * e[t][p]) * inv)
+                 for t in range(p + 2, 8)}
+            for i in later:
+                update[i] = update[i] + (column[i][p] * y0 + column[i][p + 1] * y1)
+                for t in range(p + 2, 8):
+                    column[i][t] = column[i][t] - (column[i][p] * f[t][0] + column[i][p + 1] * f[t][1])
+            for t in range(p + 2, 8):
+                row[t] = row[t] - (e[t][p] * y0 + e[t][p + 1] * y1)
+                for u in range(p + 2, t + 1):
+                    e[t][u] = e[t][u] - (e[t][p] * f[u][0] + e[t][p + 1] * f[u][1])
+        for t in range(2, 8):
+            work[b] = jnp.where(sub == t, row[t], work[b])
+        for i in later:
+            work[i] = work[i] - update[i]
 
     odd = sub % 2 == 1
     rows = []
@@ -104,7 +100,7 @@
     return high, middle, (rest - middle.astype(F32)).astype(BF16)
 
 
-def kernel(x_ref, start_ref, high, low, basis_ref, start_buf, buf, gram, pair, zacc, g3, zsend, zslots, zz, zall,
+def kernel(x_ref, start_ref, high, low, basis_ref, start_buf, buf, gram, triple, zacc, g3, zsend, zslots, zz, zall,
            start_sem, own_sem, send_sem, recv_sem, zsend_sem, rs_sem, zz_send_sem, zz_sem, ag_send_sem, ag_sem):
     w = lax.axis_index("wide")
     z = lax.axis_index("narrow")
@@ -153,7 +149,8 @@
         h, l = split(buf[s])
         high[s] = h
         low[s] = l
-        inner = jnp.concatenate(split(fold(dot(pair[...], h, exact=False) + dot(pair[...], l, exact=False))), axis=0)
+        inner = dot(triple[...], h, exact=False) + dot(triple[...], l, exact=False)
+        inner = jnp.concatenate(split(inner[:64] + (inner[64:128] + inner[128:])), axis=0)
         zacc[...] += fold(dot(inner, h, nt, False) + dot(inner, l, nt, False))
 
     def accumulate(s):
@@ -168,7 +165,7 @@
     zacc[...] = jnp.zeros_like(zacc)
     begun.wait()
     start = start_buf[...]
-    pair[...] = jnp.concatenate(split(dot(inverse_of(start), start)), axis=0)
+    triple[...] = jnp.concatenate(split3(dot(inverse_of(start), start)), axis=0)
     own.wait()
 
     @pl.loop(0, spectra - AHEAD)
@@ -267,7 +264,7 @@
             pltpu.VMEM((64, 512), F32),
             pltpu.VMEM((spectra, 512, cols), F32),
             pltpu.VMEM((512, 512), F32),
-            pltpu.VMEM((128, 512), BF16),
+            pltpu.VMEM((192, 512), BF16),
             pltpu.VMEM((64, 512), F32),
             pltpu.VMEM((3, 512, 512), BF16),
             pltpu.VMEM((ITERS, 64, 512), F32),

time: 187 us -> 183 us (0.979)
  Pallas kernels: 185 us -> 183 us
    pallas_call x1, Pallas kernels: 182 us -> 179 us  [on_device(): pl.pallas_call(kernel, out_shape=(pltpu.VMEM((spectra, 512, cols), BF16),...]
where the time goes in v3:
time: 183 us
  Pallas kernels  183 us (100%)
    pallas_call x1, Pallas kernels, on_device(): pl.pallas_call(kernel, out_shape=(pltpu.VMEM((spectra, 512, cols), BF16),...  179 us

profile of v3, /device:TPU:1, one launch (start us, length us, event | category | flops | bytes accessed | tf_op | source)
XLA Modules:
  0.0 183.3 jit_solution(14128957075208726836)
XLA Ops:
  0.6 179.3 %shard_map.41 = (bf16[24,512,256]{2,1,0:T(8,128)(2,1)S(1)}, bf16[24,512,256]{2,1,0:T(8,128)(2,1)S(1)}, f32[64,512]{1,0:T(8,128)S(1)}) custom-call(f32[24,16,8192]{2,1,0:T(8,128)} %x_ref.1, f32[64,512]{1,0:T(8,128)} %bitcast.2), custom_call_target="tpu_custom_call" | custom-call | tf_op jit(solution)/shard_map/pallas_call | solution.py:257
  179.9 3.4 %shard_map.42 = (f32[24,64,256]{2,1,0:T(8,128)}, f32[64,512]{1,0:T(8,128)}) custom-call(bf16[24,512,256]{2,1,0:T(8,128)(2,1)S(1)} %get-tuple-element.7.high, bf16[24,512,256]{2,1,0:T(8,128)(2,1)S(1)} %get-tuple-element.8.low, f32[64,512]{1,0:T(8,128)S(1)} %get-tuple-element.9.basis_ref), custom_call_target="tpu_custom_call" | custom-call | tf_op jit(solution)/shard_map/pallas_call | solution.py:280

commit v4 on v3

--- a/solution.py
+++ b/solution.py
@@ -16,6 +16,9 @@
 NX, NY, CORES, NZ = 4, 4, 2, 4
 WIDE = NX * NY * CORES
 PEERS = [(y, x, c) for y in range(NY) for x in range(NX) for c in range(CORES) if (y, x, c) != (0, 0, 0)]
+
+FAR_FIRST = sorted(PEERS, key=lambda o: -min(o[0], NY - o[0]) - min(o[1], NX - o[1]))
+FAR_CHIPS = [o for o in FAR_FIRST if o[2] == 0]
 
 
 def dot(a, b, dims=((1,), (0,)), exact=True):
@@ -100,8 +103,10 @@
     return high, middle, (rest - middle.astype(F32)).astype(BF16)
 
 
-def kernel(x_ref, start_ref, high, low, basis_ref, start_buf, buf, gram, triple, zacc, g3, zsend, zslots, zz, zall,
-           start_sem, own_sem, send_sem, recv_sem, zsend_sem, rs_sem, zz_send_sem, zz_sem, ag_send_sem, ag_sem):
+def kernel(x_ref, start_ref, high, low, basis_ref, start_buf, buf, gram, triple, zacc, gram_rows, gram_other, gram_chip, gram_slots,
+           zsend, zslots, zz, zall, wall,
+           start_sem, own_sem, send_sem, recv_sem, zsend_sem, rs_sem, zz_send_sem, zz_sem, ag_send_sem, ag_sem,
+           pair_send_sem, pair_sem, rows_send_sem, rows_sem):
     w = lax.axis_index("wide")
     z = lax.axis_index("narrow")
     cc, xx, yy = lax.rem(w, CORES), lax.rem(w // CORES, NX), w // (CORES * NX)
@@ -112,7 +117,7 @@
         return (lax.rem(yy + y, NY) * NX + lax.rem(xx + x, NX)) * CORES + lax.rem(cc + c, CORES)
 
     peers = [peer(offset) for offset in PEERS]
-    far_first = [peer(offset) for offset in sorted(PEERS, key=lambda o: -min(o[0], NY - o[0]) - min(o[1], NX - o[1]))]
+    far_first = [peer(offset) for offset in FAR_FIRST]
     depths = [lax.rem(z + d, NZ) for d in (2, 1, 3)]
 
     barrier = pltpu.get_barrier_semaphore()
@@ -184,53 +189,66 @@
     def tile(ref, t):
         return ref.at[pl.ds(pl.multiple_of(t // 4 * 8, 8), 8), pl.ds(pl.multiple_of(lax.rem(t, 4) * 128, 128), 128)]
 
-    def reduce(it, value):
-        zsend[it] = value
-        for t in far_first:
-            pltpu.make_async_remote_copy(
-                src_ref=tile(zsend.at[it], t), dst_ref=zslots.at[it, w],
-                send_sem=zsend_sem.at[it], recv_sem=rs_sem.at[it], device_id=(t, z), device_id_type=MESH).start()
-        zslots[it, w] = tile(zsend.at[it], w)[...]
-
-    def spread(it):
-        arrived(zslots.at[it, pl.ds(0, len(PEERS))], rs_sem.at[it])
-        zz[it, z] = jnp.sum(zslots[it], axis=0)
+    def swap_planes(it, value):
+        zz[it, z] = value
         for d in depths:
             pltpu.make_async_remote_copy(
                 src_ref=zz.at[it, z], dst_ref=zz.at[it, z],
                 send_sem=zz_send_sem.at[it], recv_sem=zz_sem.at[it], device_id=(w, d), device_id_type=MESH).start()
+
+    def spread(it, place):
         arrived(zz.at[it, pl.ds(0, len(depths))], zz_sem.at[it])
-        tile(zall.at[it], w)[...] = (zz[it, 0] + zz[it, 1]) + (zz[it, 2] + zz[it, 3])
+        place[...] = (zz[it, 0] + zz[it, 1]) + (zz[it, 2] + zz[it, 3])
         for t in far_first:
             pltpu.make_async_remote_copy(
-                src_ref=tile(zall.at[it], w), dst_ref=tile(zall.at[it], w),
+                src_ref=place, dst_ref=place,
                 send_sem=ag_send_sem.at[it], recv_sem=ag_sem.at[it], device_id=(t, z), device_id_type=MESH).start()
 
-    def gathered(it):
-        arrived(zslots.at[it, pl.ds(0, len(PEERS))], ag_sem.at[it])
-        return zall[it]
-
-    reduce(0, zacc[...])
+    zsend[...] = zacc[...]
+    for t in far_first:
+        pltpu.make_async_remote_copy(
+            src_ref=tile(zsend, t), dst_ref=zslots.at[w],
+            send_sem=zsend_sem, recv_sem=rs_sem, device_id=(t, z), device_id_type=MESH).start()
+    zslots[w] = tile(zsend, w)[...]
+
     accumulate(spectra - 1)
-    for i, g in enumerate(split3(gram[...])):
-        g3[i] = g
-    spread(0)
-    z1 = gathered(0)
-    zh, zm, zl = split3(z1)
-    by_high = dot(jnp.concatenate([zh, zm, zl], axis=0), g3[0], exact=False)
-    by_middle = dot(jnp.concatenate([zh, zm], axis=0), g3[1], exact=False)
-    by_low = dot(zh, g3[2], exact=False)
-    reduce(1, by_high[:64] + ((by_high[64:128] + by_middle[:64]) + ((by_high[128:] + by_middle[64:]) + by_low)))
+    gram_rows[...] = gram[...].reshape(gram_rows.shape)
+    other = peer((0, 0, 1))
+    pltpu.make_async_remote_copy(
+        src_ref=gram_rows.at[:, :, 1 - cc], dst_ref=gram_other,
+        send_sem=pair_send_sem, recv_sem=pair_sem, device_id=(other, z), device_id_type=MESH).start()
+    arrived(gram_other, pair_sem)
+    gram_chip[...] = gram_rows[:, :, cc] + gram_other[...]
+    chip = w // CORES
+    for offset in FAR_CHIPS:
+        t = peer(offset)
+        pltpu.make_async_remote_copy(
+            src_ref=gram_chip.at[:, t // CORES], dst_ref=gram_slots.at[chip],
+            send_sem=rows_send_sem, recv_sem=rows_sem, device_id=(t, z), device_id_type=MESH).start()
+    gram_slots[chip] = gram_chip[:, chip]
+
+    arrived(zslots.at[pl.ds(0, len(PEERS))], rs_sem)
+    swap_planes(0, jnp.sum(zslots[...], axis=0))
+    spread(0, tile(zall, w))
+    arrived(zslots.at[pl.ds(0, len(PEERS))], ag_sem.at[0])
+    z1 = zall[...]
+
+    arrived(gram_slots.at[pl.ds(0, len(FAR_CHIPS))], rows_sem)
+    mine = dot(jnp.sum(gram_slots[...], axis=0).reshape(16, 512), z1, nt)
+    swap_planes(1, jnp.concatenate([mine[:8], mine[8:]], axis=1))
     inv1 = inverse_of(z1)
-    spread(1)
-    z2 = dot(inv1, gathered(1))
+    spread(1, wall.at[pl.ds(pl.multiple_of(w * 8, 8), 8), :])
+    arrived(zslots.at[pl.ds(0, len(PEERS))], ag_sem.at[1])
+    z2 = jnp.concatenate([dot(inv1, wall[:, :64], nt), dot(inv1, wall[:, 64:], nt)], axis=1)
     basis_ref[...] = dot(inverse_of(z2), z2)
 
     arrived(buf.at[:, pl.ds(0, len(PEERS) * rows), :], send_sem)
+    arrived(zslots.at[pl.ds(0, len(PEERS))], zsend_sem)
+    arrived(gram_other, pair_send_sem)
+    arrived(gram_slots.at[pl.ds(0, len(FAR_CHIPS))], rows_send_sem)
     for it in range(ITERS):
-        arrived(zslots.at[it, pl.ds(0, len(PEERS))], zsend_sem.at[it])
         arrived(zz.at[it, pl.ds(0, len(depths))], zz_send_sem.at[it])
-        arrived(zslots.at[it, pl.ds(0, len(PEERS))], ag_send_sem.at[it])
+        arrived(zslots.at[pl.ds(0, len(PEERS))], ag_send_sem.at[it])
 
 
 def project(high, low, basis_ref, core_ref, factor_ref):
@@ -266,13 +284,18 @@
             pltpu.VMEM((512, 512), F32),
             pltpu.VMEM((192, 512), BF16),
             pltpu.VMEM((64, 512), F32),
-            pltpu.VMEM((3, 512, 512), BF16),
-            pltpu.VMEM((ITERS, 64, 512), F32),
-            pltpu.VMEM((ITERS, WIDE, 8, 128), F32),
+            pltpu.VMEM((2, WIDE // CORES, CORES, 8, 512), F32),
+            pltpu.VMEM((2, WIDE // CORES, 8, 512), F32),
+            pltpu.VMEM((2, WIDE // CORES, 8, 512), F32),
+            pltpu.VMEM((WIDE // CORES, 2, 8, 512), F32),
+            pltpu.VMEM((64, 512), F32),
+            pltpu.VMEM((WIDE, 8, 128), F32),
             pltpu.VMEM((ITERS, NZ, 8, 128), F32),
-            pltpu.VMEM((ITERS, 64, 512), F32),
+            pltpu.VMEM((64, 512), F32),
+            pltpu.VMEM((256, 128), F32),
             dma(()), dma(()), dma(()), dma((spectra,)),
-            dma((ITERS,)), dma((ITERS,)), dma((ITERS,)), dma((ITERS,)), dma((ITERS,)), dma((ITERS,)),
+            dma(()), dma(()), dma((ITERS,)), dma((ITERS,)), dma((ITERS,)), dma((ITERS,)),
+            dma(()), dma(()), dma(()), dma(()),
         ],
         compiler_params=pltpu.CompilerParams(
             collective_id=0, has_side_effects=True, vmem_limit_bytes=KERNEL_VMEM),

time: 183 us -> 179 us (0.978)
  Pallas kernels: 183 us -> 179 us
    pallas_call x1, Pallas kernels: 179 us -> 175 us  [on_device(): pl.pallas_call(kernel, out_shape=(pltpu.VMEM((spectra, 512, cols), BF16),...]
where the time goes in v4:
time: 179 us
  Pallas kernels  179 us (100%)
    pallas_call x1, Pallas kernels, on_device(): pl.pallas_call(kernel, out_shape=(pltpu.VMEM((spectra, 512, cols), BF16),...  175 us

profile of v4, /device:TPU:1, one launch (start us, length us, event | category | flops | bytes accessed | tf_op | source)
XLA Modules:
  0.0 179.4 jit_solution(12217204855932509814)
XLA Ops:
  0.6 175.4 %shard_map.41 = (bf16[24,512,256]{2,1,0:T(8,128)(2,1)S(1)}, bf16[24,512,256]{2,1,0:T(8,128)(2,1)S(1)}, f32[64,512]{1,0:T(8,128)S(1)}) custom-call(f32[24,16,8192]{2,1,0:T(8,128)} %x_ref.1, f32[64,512]{1,0:T(8,128)} %bitcast.2), custom_call_target="tpu_custom_call" | custom-call | tf_op jit(solution)/shard_map/pallas_call | solution.py:275
  176.0 3.4 %shard_map.42 = (f32[24,64,256]{2,1,0:T(8,128)}, f32[64,512]{1,0:T(8,128)}) custom-call(bf16[24,512,256]{2,1,0:T(8,128)(2,1)S(1)} %get-tuple-element.7.high, bf16[24,512,256]{2,1,0:T(8,128)(2,1)S(1)} %get-tuple-element.8.low, f32[64,512]{1,0:T(8,128)S(1)} %get-tuple-element.9.basis_ref), custom_call_target="tpu_custom_call" | custom-call | tf_op jit(solution)/shard_map/pallas_call | solution.py:303

commit v5 on v4

--- a/solution.py
+++ b/solution.py
@@ -103,10 +103,10 @@
     return high, middle, (rest - middle.astype(F32)).astype(BF16)
 
 
-def kernel(x_ref, start_ref, high, low, basis_ref, start_buf, buf, gram, triple, zacc, gram_rows, gram_other, gram_chip, gram_slots,
+def kernel(x_ref, start_ref, high, low, basis_ref, start_buf, buf, gram, triple, zacc, gram_rows, gram_other, gram_chip, gram_slots, gram_planes,
            zsend, zslots, zz, zall, wall,
            start_sem, own_sem, send_sem, recv_sem, zsend_sem, rs_sem, zz_send_sem, zz_sem, ag_send_sem, ag_sem,
-           pair_send_sem, pair_sem, rows_send_sem, rows_sem):
+           pair_send_sem, pair_sem, rows_send_sem, rows_sem, planes_send_sem, planes_sem):
     w = lax.axis_index("wide")
     z = lax.axis_index("narrow")
     cc, xx, yy = lax.rem(w, CORES), lax.rem(w // CORES, NX), w // (CORES * NX)
@@ -189,16 +189,18 @@
     def tile(ref, t):
         return ref.at[pl.ds(pl.multiple_of(t // 4 * 8, 8), 8), pl.ds(pl.multiple_of(lax.rem(t, 4) * 128, 128), 128)]
 
-    def swap_planes(it, value):
-        zz[it, z] = value
+    def swap_planes(ref, sends, sem):
         for d in depths:
             pltpu.make_async_remote_copy(
-                src_ref=zz.at[it, z], dst_ref=zz.at[it, z],
-                send_sem=zz_send_sem.at[it], recv_sem=zz_sem.at[it], device_id=(w, d), device_id_type=MESH).start()
-
-    def spread(it, place):
-        arrived(zz.at[it, pl.ds(0, len(depths))], zz_sem.at[it])
-        place[...] = (zz[it, 0] + zz[it, 1]) + (zz[it, 2] + zz[it, 3])
+                src_ref=ref.at[z], dst_ref=ref.at[z],
+                send_sem=sends, recv_sem=sem, device_id=(w, d), device_id_type=MESH).start()
+
+    def four_planes(ref, sem):
+        arrived(ref.at[pl.ds(0, len(depths))], sem)
+        return (ref[0] + ref[1]) + (ref[2] + ref[3])
+
+    def spread(it, place, value):
+        place[...] = value
         for t in far_first:
             pltpu.make_async_remote_copy(
                 src_ref=place, dst_ref=place,
@@ -228,26 +230,32 @@
     gram_slots[chip] = gram_chip[:, chip]
 
     arrived(zslots.at[pl.ds(0, len(PEERS))], rs_sem)
-    swap_planes(0, jnp.sum(zslots[...], axis=0))
-    spread(0, tile(zall, w))
+    zz[z] = jnp.sum(zslots[...], axis=0)
+    swap_planes(zz, zz_send_sem, zz_sem)
+    spread(0, tile(zall, w), four_planes(zz, zz_sem))
+
+    arrived(gram_slots.at[pl.ds(0, len(FAR_CHIPS))], rows_sem)
+    gram_planes[z] = jnp.sum(gram_slots[...], axis=0)
+    swap_planes(gram_planes, planes_send_sem, planes_sem)
+
     arrived(zslots.at[pl.ds(0, len(PEERS))], ag_sem.at[0])
     z1 = zall[...]
 
-    arrived(gram_slots.at[pl.ds(0, len(FAR_CHIPS))], rows_sem)
-    mine = dot(jnp.sum(gram_slots[...], axis=0).reshape(16, 512), z1, nt)
-    swap_planes(1, jnp.concatenate([mine[:8], mine[8:]], axis=1))
-    inv1 = inverse_of(z1)
-    spread(1, wall.at[pl.ds(pl.multiple_of(w * 8, 8), 8), :])
+    b1 = dot(inverse_of(z1), z1)
+    mine = dot(four_planes(gram_planes, planes_sem).reshape(16, 512), b1, nt)
+    spread(1, wall.at[pl.ds(pl.multiple_of(w * 8, 8), 8), :], jnp.concatenate([mine[:8], mine[8:]], axis=1))
     arrived(zslots.at[pl.ds(0, len(PEERS))], ag_sem.at[1])
-    z2 = jnp.concatenate([dot(inv1, wall[:, :64], nt), dot(inv1, wall[:, 64:], nt)], axis=1)
+    halves = wall[...].T
+    z2 = jnp.concatenate([halves[:64], halves[64:]], axis=1)
     basis_ref[...] = dot(inverse_of(z2), z2)
 
     arrived(buf.at[:, pl.ds(0, len(PEERS) * rows), :], send_sem)
     arrived(zslots.at[pl.ds(0, len(PEERS))], zsend_sem)
     arrived(gram_other, pair_send_sem)
     arrived(gram_slots.at[pl.ds(0, len(FAR_CHIPS))], rows_send_sem)
+    arrived(zz.at[pl.ds(0, len(depths))], zz_send_sem)
+    arrived(gram_planes.at[pl.ds(0, len(depths))], planes_send_sem)
     for it in range(ITERS):
-        arrived(zz.at[it, pl.ds(0, len(depths))], zz_send_sem.at[it])
         arrived(zslots.at[pl.ds(0, len(PEERS))], ag_send_sem.at[it])
 
 
@@ -288,14 +296,15 @@
             pltpu.VMEM((2, WIDE // CORES, 8, 512), F32),
             pltpu.VMEM((2, WIDE // CORES, 8, 512), F32),
             pltpu.VMEM((WIDE // CORES, 2, 8, 512), F32),
+            pltpu.VMEM((NZ, 2, 8, 512), F32),
             pltpu.VMEM((64, 512), F32),
             pltpu.VMEM((WIDE, 8, 128), F32),
-            pltpu.VMEM((ITERS, NZ, 8, 128), F32),
+            pltpu.VMEM((NZ, 8, 128), F32),
             pltpu.VMEM((64, 512), F32),
             pltpu.VMEM((256, 128), F32),
             dma(()), dma(()), dma(()), dma((spectra,)),
-            dma(()), dma(()), dma((ITERS,)), dma((ITERS,)), dma((ITERS,)), dma((ITERS,)),
-            dma(()), dma(()), dma(()), dma(()),
+            dma(()), dma(()), dma(()), dma(()), dma((ITERS,)), dma((ITERS,)),
+            dma(()), dma(()), dma(()), dma(()), dma(()), dma(()),
         ],
         compiler_params=pltpu.CompilerParams(
             collective_id=0, has_side_effects=True, vmem_limit_bytes=KERNEL_VMEM),

time: 179 us -> 177 us (0.989)
  Pallas kernels: 179 us -> 176 us
    pallas_call x1, Pallas kernels: 175 us -> 173 us  [on_device(): pl.pallas_call(kernel, out_shape=(pltpu.VMEM((spectra, 512, cols), BF16),...]
where the time goes in v5:
time: 177 us
  Pallas kernels  176 us (99%)
    pallas_call x1, Pallas kernels, on_device(): pl.pallas_call(kernel, out_shape=(pltpu.VMEM((spectra, 512, cols), BF16),...  173 us

profile of v5, /device:TPU:1, one launch (start us, length us, event | category | flops | bytes accessed | tf_op | source)
XLA Modules:
  0.0 176.7 jit_solution(5888817838391992782)
XLA Ops:
  0.6 172.7 %shard_map.41 = (bf16[24,512,256]{2,1,0:T(8,128)(2,1)S(1)}, bf16[24,512,256]{2,1,0:T(8,128)(2,1)S(1)}, f32[64,512]{1,0:T(8,128)S(1)}) custom-call(f32[24,16,8192]{2,1,0:T(8,128)} %x_ref.1, f32[64,512]{1,0:T(8,128)} %bitcast.2), custom_call_target="tpu_custom_call" | custom-call | tf_op jit(solution)/shard_map/pallas_call | solution.py:283
  173.3 3.4 %shard_map.42 = (f32[24,64,256]{2,1,0:T(8,128)}, f32[64,512]{1,0:T(8,128)}) custom-call(bf16[24,512,256]{2,1,0:T(8,128)(2,1)S(1)} %get-tuple-element.7.high, bf16[24,512,256]{2,1,0:T(8,128)(2,1)S(1)} %get-tuple-element.8.low, f32[64,512]{1,0:T(8,128)S(1)} %get-tuple-element.9.basis_ref), custom_call_target="tpu_custom_call" | custom-call | tf_op jit(solution)/shard_map/pallas_call | solution.py:312

commit v6 on v5

--- a/solution.py
+++ b/solution.py
@@ -9,7 +9,7 @@
 F32, BF16 = jnp.float32, jnp.bfloat16
 ITERS = 2
 AHEAD = 8
-PARTS = 2
+PARTS = 1
 GROUP = 8
 KERNEL_VMEM = 52953088
 PROJECT_VMEM = 8 * 2**20
@@ -138,7 +138,7 @@
     def send(s):
         for r in range(PARTS):
             here = pl.ds(pl.multiple_of(w * rows + r * part, part), part)
-            for t in peers:
+            for t in far_first:
                 pltpu.make_async_remote_copy(
                     src_ref=x_ref.at[s, pl.ds(r * part, part), pl.ds(pl.multiple_of(t * cols, cols), cols)],
                     dst_ref=buf.at[s, here, :],

time: 177 us -> 176 us (level)
  no operation moved by 1% of the time
where the time goes in v6:
time: 176 us
  Pallas kernels  175 us (99%)
    pallas_call x1, Pallas kernels, on_device(): pl.pallas_call(kernel, out_shape=(pltpu.VMEM((spectra, 512, cols), BF16),...  172 us

profile of v6, /device:TPU:1, one launch (start us, length us, event | category | flops | bytes accessed | tf_op | source)
XLA Modules:
  0.0 175.8 jit_solution(1619864136858959959)
XLA Ops:
  0.6 171.8 %shard_map.41 = (bf16[24,512,256]{2,1,0:T(8,128)(2,1)S(1)}, bf16[24,512,256]{2,1,0:T(8,128)(2,1)S(1)}, f32[64,512]{1,0:T(8,128)S(1)}) custom-call(f32[24,16,8192]{2,1,0:T(8,128)} %x_ref.1, f32[64,512]{1,0:T(8,128)} %bitcast.2), custom_call_target="tpu_custom_call" | custom-call | tf_op jit(solution)/shard_map/pallas_call | solution.py:283
  172.5 3.4 %shard_map.42 = (f32[24,64,256]{2,1,0:T(8,128)}, f32[64,512]{1,0:T(8,128)}) custom-call(bf16[24,512,256]{2,1,0:T(8,128)(2,1)S(1)} %get-tuple-element.7.high, bf16[24,512,256]{2,1,0:T(8,128)(2,1)S(1)} %get-tuple-element.8.low, f32[64,512]{1,0:T(8,128)S(1)} %get-tuple-element.9.basis_ref), custom_call_target="tpu_custom_call" | custom-call | tf_op jit(solution)/shard_map/pallas_call | solution.py:312

commit v7 on v6

--- a/solution.py
+++ b/solution.py
@@ -10,7 +10,7 @@
 ITERS = 2
 AHEAD = 8
 PARTS = 1
-GROUP = 8
+GROUP = 12
 KERNEL_VMEM = 52953088
 PROJECT_VMEM = 8 * 2**20
 NX, NY, CORES, NZ = 4, 4, 2, 4

time: 176 us -> 176 us (level)
  no operation moved by 1% of the time
where the time goes in v7:
time: 176 us
  Pallas kernels  175 us (99%)
    pallas_call x1, Pallas kernels, on_device(): pl.pallas_call(kernel, out_shape=(pltpu.VMEM((spectra, 512, cols), BF16),...  172 us

profile of v7, /device:TPU:1, one launch (start us, length us, event | category | flops | bytes accessed | tf_op | source)
XLA Modules:
  0.0 175.8 jit_solution(13185458836948999796)
XLA Ops:
  0.6 171.8 %shard_map.41 = (bf16[24,512,256]{2,1,0:T(8,128)(2,1)S(1)}, bf16[24,512,256]{2,1,0:T(8,128)(2,1)S(1)}, f32[64,512]{1,0:T(8,128)S(1)}) custom-call(f32[24,16,8192]{2,1,0:T(8,128)} %x_ref.1, f32[64,512]{1,0:T(8,128)} %bitcast.2), custom_call_target="tpu_custom_call" | custom-call | tf_op jit(solution)/shard_map/pallas_call | solution.py:283
  172.5 3.3 %shard_map.42 = (f32[24,64,256]{2,1,0:T(8,128)}, f32[64,512]{1,0:T(8,128)}) custom-call(bf16[24,512,256]{2,1,0:T(8,128)(2,1)S(1)} %get-tuple-element.7.high, bf16[24,512,256]{2,1,0:T(8,128)(2,1)S(1)} %get-tuple-element.8.low, f32[64,512]{1,0:T(8,128)S(1)} %get-tuple-element.9.basis_ref), custom_call_target="tpu_custom_call" | custom-call | tf_op jit(solution)/shard_map/pallas_call | solution.py:312
